TPU v7x, 32 devices: a whole 2x2x4 slice. The times are simulated.
32 devices in a mesh: dp: 8 (over y, x, core), mp: 4 (over z).
Axes of the slice: x: 2, y: 2, z: 4, core: 2. Of those that a mesh axis runs over, the one named last changes fastest.
Arguments:
- buffer: bfloat16 [65536, 256], P(('dp', 'mp')), may hold values from -24 to 24, as said below
- owner: int32 [32768, 1], P(('dp', 'mp')), may hold values from 0 to 31; in each aligned block of 1024 rows (0 to 1023, 1024 to 2047, ...) at most 128 rows name the same one
- local_row: int32 [32768], P(('dp', 'mp')), may hold values from 0 to 2047
- q_in: bfloat16 [2, 130, 256], replicated, may hold values from -0.5 to 0.5
- q_mid: bfloat16 [2, 256, 256], replicated, may hold values from -0.5 to 0.5
- q_out: bfloat16 [2, 256], replicated, may hold values from -0.5 to 0.5
- v_in: bfloat16 [124, 256], replicated, may hold values from -0.5 to 0.5
- v_mid: bfloat16 [256, 256], replicated, may hold values from -0.5 to 0.5
- v_out: bfloat16 [256], replicated, may hold values from -0.5 to 0.5
Outputs:
- q_values: float32 [2, 32768], P(None, ('dp', 'mp'))
- values: float32 [2, 32768], P(None, ('dp', 'mp'))
- targets: float32 [32768], P(('dp', 'mp'))
- q_loss: float32 [32768], P(('dp', 'mp'))
- value_loss: float32 [32768], P(('dp', 'mp'))
Inputs may be any that keep to these rules, and one draw needn't show every extreme that they name: Owner o is the replay owner at position o of the devices in dp+mp order. In the rows of one reader no owner is named more than 128 times, a bound that some block reaches. `buffer`: action values lie in -1 to 1 and discounts in 0 to 0.99.
All inputs are finite; a program needn't handle non-finite values.
Results may differ from a plain program's by a relative error of at most 0.005.
Values may be sent and summed in bfloat16 or wider, within the bound.
A program may use at most 64 MiB of HBM per device.

v0:
```python
import jax
import jax.numpy as jnp
from jax import lax
from jax.sharding import PartitionSpec as P


def layer_two(first, mid, out):
    hidden = jnp.maximum(jnp.dot(first, mid, preferred_element_type=jnp.float32), 0.0)
    return jnp.dot(hidden, out.astype(jnp.float32), precision=lax.Precision.HIGHEST)


def critic_block(rows, weights, states_width, pair_width):
    q_in, q_mid, q_out, v_in, v_mid, v_out = weights
    pair = rows[:, :pair_width]
    state = rows[:, :states_width]
    nexts = rows[:, pair_width : pair_width + states_width]
    reward = rows[:, pair_width + states_width].astype(jnp.float32)
    discount = rows[:, pair_width + states_width + 1].astype(jnp.float32)
    first_one = jnp.maximum(jnp.dot(pair, q_in[0], preferred_element_type=jnp.float32), 0.0).astype(
        jnp.bfloat16
    )
    first_two = jnp.maximum(jnp.dot(pair, q_in[1], preferred_element_type=jnp.float32), 0.0).astype(
        jnp.bfloat16
    )
    q_first = layer_two(first_one, q_mid[0], q_out[0])
    q_second = layer_two(first_two, q_mid[1], q_out[1])
    both = jnp.concatenate([state, nexts], axis=0)
    first_value = jnp.maximum(jnp.dot(both, v_in, preferred_element_type=jnp.float32), 0.0).astype(
        jnp.bfloat16
    )
    value_all = layer_two(first_value, v_mid, v_out)
    count = state.shape[0]
    value_now = value_all[:count]
    value_next = value_all[count:]
    targets = reward + discount * value_next
    return (q_first, q_second, value_now, value_next, targets)


def body(buffer, owner, local_row, q_in, q_mid, q_out, v_in, v_mid, v_out):
    outer = lax.axis_size("dp")
    inner = lax.axis_size("mp")
    owners = outer * inner
    batch = local_row.shape[0]
    columns_all = buffer.shape[1]
    states_width = v_in.shape[0]
    pair_width = q_in.shape[1]
    weights = (q_in, q_mid, q_out, v_in, v_mid, v_out)
    slots_each = max(2, 4 * batch // owners)
    target_owner = owner[:, 0]
    positions = jnp.arange(batch, dtype=jnp.int32)
    same_owner = target_owner[:, None] == target_owner[None, :]
    earlier = positions[None, :] < positions[:, None]
    placed = jnp.sum(jnp.logical_and(same_owner, earlier).astype(jnp.int32), axis=1)
    owner_hot = (target_owner[:, None] == jnp.arange(owners, dtype=jnp.int32)[None, :]).astype(
        jnp.float32
    )
    place_hot = (placed[:, None] == jnp.arange(slots_each, dtype=jnp.int32)[None, :]).astype(
        jnp.float32
    )
    weighted = place_hot * (local_row.astype(jnp.float32) + 1.0)[:, None]
    table = jnp.dot(owner_hot.T, weighted, precision=lax.Precision.HIGHEST)
    requests = (table.astype(jnp.int32) - 1).reshape(outer, inner, slots_each)
    asked = lax.all_to_all(
        lax.all_to_all(requests, "dp", split_axis=0, concat_axis=0, tiled=True),
        "mp",
        split_axis=1,
        concat_axis=1,
        tiled=True,
    )
    picked = jnp.take(buffer, jnp.maximum(asked, 0).reshape(-1), axis=0)

    def evaluate(block):
        return jnp.stack(critic_block(block, weights, states_width, pair_width))

    served = lax.map(evaluate, picked.reshape(outer, inner * slots_each, columns_all))
    served = served.reshape(outer, 5, inner, slots_each)
    returned = lax.all_to_all(
        lax.all_to_all(served, "dp", split_axis=0, concat_axis=0, tiled=True),
        "mp",
        split_axis=2,
        concat_axis=2,
        tiled=True,
    )
    flat = jnp.transpose(returned, (1, 0, 2, 3)).reshape(5, owners, slots_each)
    by_slot = jnp.einsum("kos,bs->kob", flat, place_hot, precision=lax.Precision.HIGHEST)
    mine = jnp.einsum("kob,bo->kb", by_slot, owner_hot, precision=lax.Precision.HIGHEST)
    q_first, q_second, value_now, value_next, targets = (
        mine[0],
        mine[1],
        mine[2],
        mine[3],
        mine[4],
    )
    q_loss = (q_first - targets) ** 2 + (q_second - targets) ** 2
    gap = jnp.minimum(q_first, q_second) - value_now
    value_loss = jnp.where(gap < 0.0, 0.3, 0.7) * gap * gap
    return (
        jnp.stack([q_first, q_second]),
        jnp.stack([value_now, value_next]),
        targets,
        q_loss,
        value_loss,
    )


def solution(mesh):
    return jax.shard_map(
        body,
        mesh=mesh,
        in_specs=(
            P(("dp", "mp"), None),
            P(("dp", "mp"), None),
            P(("dp", "mp")),
            P(),
            P(),
            P(),
            P(),
            P(),
            P(),
        ),
        out_specs=(
            P(None, ("dp", "mp")),
            P(None, ("dp", "mp")),
            P(("dp", "mp")),
            P(("dp", "mp")),
            P(("dp", "mp")),
        ),
        check_vma=False,
    )
```

profile of v0, /device:TPU:0, one launch (start us, length us, event | category | flops | bytes accessed | tf_op | source)
XLA Modules:
  0.0 118.4 jit_solution(8527828568259253387)
XLA Ops:
  0.6 1.3 %convert_reduce_fusion = s32[1024]{0:T(1024)S(1)} fusion(s32[1024]{0:T(1024)} %bitcast.125), kind=kLoop, calls=%fused_computation.40 | loop fusion | flops 5241856 | bytes 8192 | tf_op jit(solution)/shard_map/reduce_sum | solution.py:53
  2.7 1.7 %fusion.42 = s32[32,128]{1,0:T(8,128)S(1)} fusion(f32[1024]{0:T(1024)S(1)} %convert_add_fusion, s32[1024]{0:T(1024)S(1)} %convert_reduce_fusion, s32[1024]{0:T(1024)} %bitcast.126), kind=kOutput, calls=%fused_computation.48 | convolution fusion | flops 50634752 | bytes 28672 | tf_op jit(solution)/shard_map/dot_general | solution.py:61
  4.4 9.8 %all_to_all.20 = s32[8,4,128]{2,1,0:T(4,128)S(1)} all-to-all(s32[8,4,128]{2,1,0:T(4,128)S(1)} %bitcast.119), channel_id=1, replica_groups=mesh['dp'=8,'mp'=4] {'dp'}, dimensions={0} | all-to-all | bytes 32768 | tf_op jit(solution)/shard_map/all_to_all | solution.py:64
  14.8 4.9 %all-to-all-start.1 = ((s32[8,4,128]{2,0,1:T(8,128)}), s32[8,4,128]{2,0,1:T(8,128)S(1)}, u32[]{:S(2)}, u32[]{:S(2)}) async-start(s32[8,4,128]{2,0,1:T(8,128)} %copy.41), calls=%async_computation.1 | async-start | bytes 32768 | tf_op jit(solution)/shard_map/all_to_all | solution.py:63
  20.6 4.7 %all-to-all-done.1 = s32[8,4,128]{2,0,1:T(8,128)S(1)} async-done(((s32[8,4,128]{2,0,1:T(8,128)}), s32[8,4,128]{2,0,1:T(8,128)S(1)}, u32[]{:S(2)}, u32[]{:S(2)}) %all-to-all-start.1) | async-done | bytes 16416 | tf_op jit(solution)/shard_map/all_to_all | solution.py:63
  25.3 16.9 %gather_fusion = bf16[4096,256]{1,0:T(8,128)(2,1)} fusion(bf16[2048,256]{1,0:T(8,128)(2,1)S(1)} %copy-done, s32[4096]{0:T(1024)S(1)} %broadcast_clamp_fusion), kind=kCustom, calls=%fused_computation | custom fusion | bytes 4210688 | tf_op jit(solution)/shard_map/jit(_take)/gather | solution.py:70
  42.3 2.9 %copy.43 = bf16[8,512,256]{1,2,0:T(8,128)(2,1)S(1)} copy(bf16[8,512,256]{2,1,0:T(8,128)(2,1)} %bitcast.104) | data formatting | bytes 4194304 | tf_op jit(solution)/shard_map/jit(_take)/gather | solution.py:70
  45.2 1.5 %broadcast_select_fusion = bf16[8,512,256]{1,2,0:T(8,128)(2,1)} fusion(bf16[8,512,256]{1,2,0:T(8,128)(2,1)S(1)} %copy.43, pred[8,512]{1,0:T(8,128)(4,1)S(1)} %compare_and_fusion), kind=kLoop, calls=%fused_computation.43 | loop fusion | flops 1048576 | bytes 4198400 | tf_op jit(solution)/shard_map/jit(_take)/select_n | solution.py:70
  46.7 51.7 %while.10 = (s32[]{:T(128)}, f32[8,5,512]{2,0,1:T(8,128)}, bf16[8,512,256]{1,2,0:T(8,128)(2,1)}, bf16[2,130,256]{2,1,0:T(8,128)(2,1)S(1)}, bf16[2,256,256]{2,1,0...) while((s32[]{:T(128)}, f32[8,5,512]{2,0,1:T(8,128)}, ...), condition=%wide.region_2.3_spmd, body=%wide.region_1.2_spmd.sunk | while | flops 409978880 | bytes 7499437 | solution.py:75
  46.7 1.0 dynamic-slice_bitcast_fusion.2
  47.8 1.5 %convolution_maximum_fusion.11 = f32[1024,256]{1,0:T(8,128)S(1)} fusion(bf16[256,256]{1,0:T(8,128)(2,1)} %get-tuple-element.229, bf16[124,256]{1,0:T(8,128)(2,1)} %get-tuple-element.228, bf16[512,124]{0,1:T(8,128)(2,1)S(1)} %get-tuple-element.195, bf16[512,124]{0,1:T(8,128)(2,1)S(1)} %get-tuple-element.196), kind=kOutput, calls=%fused_computation.1.clone.1 | convolution fusion | flops 200523776 | bytes 1497088 | tf_op jit(solution)/shard_map/while/body/eval_jaxpr/dot_general | solution.py:8
  51.6 1.6 %dynamic_update_slice.5 = f32[8,5,512]{2,0,1:T(8,128)} dynamic-update-slice(f32[8,5,512]{2,0,1:T(8,128)} %get-tuple-element.212, f32[1,5,512]{2,0,1:T(1,128)S(1)} %copy.60, s32[]{:T(128)} %get-tuple-element.211, s32[]{:T(128)} %constant.20.clone.1..sunk, s32[]{:T(128)} %constant.20.clone.1..sunk) | dynamic-update-slice | bytes 20484 | tf_op jit(solution)/shard_map/while/body/jit(dynamic_update_index_in_dim)/dynamic_update_slice | solution.py:75
  53.2 1.0 dynamic-slice_bitcast_fusion.2
  54.2 1.5 %convolution_maximum_fusion.11 = f32[1024,256]{1,0:T(8,128)S(1)} fusion(bf16[256,256]{1,0:T(8,128)(2,1)} %get-tuple-element.229, bf16[124,256]{1,0:T(8,128)(2,1)} %get-tuple-element.228, bf16[512,124]{0,1:T(8,128)(2,1)S(1)} %get-tuple-element.195, bf16[512,124]{0,1:T(8,128)(2,1)S(1)} %get-tuple-element.196), kind=kOutput, calls=%fused_computation.1.clone.1 | convolution fusion | flops 200523776 | bytes 1497088 | tf_op jit(solution)/shard_map/while/body/eval_jaxpr/dot_general | solution.py:8
  58.1 1.6 %dynamic_update_slice.5 = f32[8,5,512]{2,0,1:T(8,128)} dynamic-update-slice(f32[8,5,512]{2,0,1:T(8,128)} %get-tuple-element.212, f32[1,5,512]{2,0,1:T(1,128)S(1)} %copy.60, s32[]{:T(128)} %get-tuple-element.211, s32[]{:T(128)} %constant.20.clone.1..sunk, s32[]{:T(128)} %constant.20.clone.1..sunk) | dynamic-update-slice | bytes 20484 | tf_op jit(solution)/shard_map/while/body/jit(dynamic_update_index_in_dim)/dynamic_update_slice | solution.py:75
  59.6 1.0 dynamic-slice_bitcast_fusion.2
  60.7 1.5 %convolution_maximum_fusion.11 = f32[1024,256]{1,0:T(8,128)S(1)} fusion(bf16[256,256]{1,0:T(8,128)(2,1)} %get-tuple-element.229, bf16[124,256]{1,0:T(8,128)(2,1)} %get-tuple-element.228, bf16[512,124]{0,1:T(8,128)(2,1)S(1)} %get-tuple-element.195, bf16[512,124]{0,1:T(8,128)(2,1)S(1)} %get-tuple-element.196), kind=kOutput, calls=%fused_computation.1.clone.1 | convolution fusion | flops 200523776 | bytes 1497088 | tf_op jit(solution)/shard_map/while/body/eval_jaxpr/dot_general | solution.py:8
  64.5 1.6 %dynamic_update_slice.5 = f32[8,5,512]{2,0,1:T(8,128)} dynamic-update-slice(f32[8,5,512]{2,0,1:T(8,128)} %get-tuple-element.212, f32[1,5,512]{2,0,1:T(1,128)S(1)} %copy.60, s32[]{:T(128)} %get-tuple-element.211, s32[]{:T(128)} %constant.20.clone.1..sunk, s32[]{:T(128)} %constant.20.clone.1..sunk) | dynamic-update-slice | bytes 20484 | tf_op jit(solution)/shard_map/while/body/jit(dynamic_update_index_in_dim)/dynamic_update_slice | solution.py:75
  67.2 1.5 %convolution_maximum_fusion.11 = f32[1024,256]{1,0:T(8,128)S(1)} fusion(bf16[256,256]{1,0:T(8,128)(2,1)} %get-tuple-element.229, bf16[124,256]{1,0:T(8,128)(2,1)} %get-tuple-element.228, bf16[512,124]{0,1:T(8,128)(2,1)S(1)} %get-tuple-element.195, bf16[512,124]{0,1:T(8,128)(2,1)S(1)} %get-tuple-element.196), kind=kOutput, calls=%fused_computation.1.clone.1 | convolution fusion | flops 200523776 | bytes 1497088 | tf_op jit(solution)/shard_map/while/body/eval_jaxpr/dot_general | solution.py:8
  71.0 1.6 %dynamic_update_slice.5 = f32[8,5,512]{2,0,1:T(8,128)} dynamic-update-slice(f32[8,5,512]{2,0,1:T(8,128)} %get-tuple-element.212, f32[1,5,512]{2,0,1:T(1,128)S(1)} %copy.60, s32[]{:T(128)} %get-tuple-element.211, s32[]{:T(128)} %constant.20.clone.1..sunk, s32[]{:T(128)} %constant.20.clone.1..sunk) | dynamic-update-slice | bytes 20484 | tf_op jit(solution)/shard_map/while/body/jit(dynamic_update_index_in_dim)/dynamic_update_slice | solution.py:75
  73.6 1.5 %convolution_maximum_fusion.11 = f32[1024,256]{1,0:T(8,128)S(1)} fusion(bf16[256,256]{1,0:T(8,128)(2,1)} %get-tuple-element.229, bf16[124,256]{1,0:T(8,128)(2,1)} %get-tuple-element.228, bf16[512,124]{0,1:T(8,128)(2,1)S(1)} %get-tuple-element.195, bf16[512,124]{0,1:T(8,128)(2,1)S(1)} %get-tuple-element.196), kind=kOutput, calls=%fused_computation.1.clone.1 | convolution fusion | flops 200523776 | bytes 1497088 | tf_op jit(solution)/shard_map/while/body/eval_jaxpr/dot_general | solution.py:8
  77.5 1.6 %dynamic_update_slice.5 = f32[8,5,512]{2,0,1:T(8,128)} dynamic-update-slice(f32[8,5,512]{2,0,1:T(8,128)} %get-tuple-element.212, f32[1,5,512]{2,0,1:T(1,128)S(1)} %copy.60, s32[]{:T(128)} %get-tuple-element.211, s32[]{:T(128)} %constant.20.clone.1..sunk, s32[]{:T(128)} %constant.20.clone.1..sunk) | dynamic-update-slice | bytes 20484 | tf_op jit(solution)/shard_map/while/body/jit(dynamic_update_index_in_dim)/dynamic_update_slice | solution.py:75
  80.1 1.5 %convolution_maximum_fusion.11 = f32[1024,256]{1,0:T(8,128)S(1)} fusion(bf16[256,256]{1,0:T(8,128)(2,1)} %get-tuple-element.229, bf16[124,256]{1,0:T(8,128)(2,1)} %get-tuple-element.228, bf16[512,124]{0,1:T(8,128)(2,1)S(1)} %get-tuple-element.195, bf16[512,124]{0,1:T(8,128)(2,1)S(1)} %get-tuple-element.196), kind=kOutput, calls=%fused_computation.1.clone.1 | convolution fusion | flops 200523776 | bytes 1497088 | tf_op jit(solution)/shard_map/while/body/eval_jaxpr/dot_general | solution.py:8
  83.9 1.6 %dynamic_update_slice.5 = f32[8,5,512]{2,0,1:T(8,128)} dynamic-update-slice(f32[8,5,512]{2,0,1:T(8,128)} %get-tuple-element.212, f32[1,5,512]{2,0,1:T(1,128)S(1)} %copy.60, s32[]{:T(128)} %get-tuple-element.211, s32[]{:T(128)} %constant.20.clone.1..sunk, s32[]{:T(128)} %constant.20.clone.1..sunk) | dynamic-update-slice | bytes 20484 | tf_op jit(solution)/shard_map/while/body/jit(dynamic_update_index_in_dim)/dynamic_update_slice | solution.py:75
  86.5 1.5 %convolution_maximum_fusion.11 = f32[1024,256]{1,0:T(8,128)S(1)} fusion(bf16[256,256]{1,0:T(8,128)(2,1)} %get-tuple-element.229, bf16[124,256]{1,0:T(8,128)(2,1)} %get-tuple-element.228, bf16[512,124]{0,1:T(8,128)(2,1)S(1)} %get-tuple-element.195, bf16[512,124]{0,1:T(8,128)(2,1)S(1)} %get-tuple-element.196), kind=kOutput, calls=%fused_computation.1.clone.1 | convolution fusion | flops 200523776 | bytes 1497088 | tf_op jit(solution)/shard_map/while/body/eval_jaxpr/dot_general | solution.py:8
  90.4 1.6 %dynamic_update_slice.5 = f32[8,5,512]{2,0,1:T(8,128)} dynamic-update-slice(f32[8,5,512]{2,0,1:T(8,128)} %get-tuple-element.212, f32[1,5,512]{2,0,1:T(1,128)S(1)} %copy.60, s32[]{:T(128)} %get-tuple-element.211, s32[]{:T(128)} %constant.20.clone.1..sunk, s32[]{:T(128)} %constant.20.clone.1..sunk) | dynamic-update-slice | bytes 20484 | tf_op jit(solution)/shard_map/while/body/jit(dynamic_update_index_in_dim)/dynamic_update_slice | solution.py:75
  91.9 1.0 dynamic-slice_bitcast_fusion.2
  93.0 1.5 %convolution_maximum_fusion.11 = f32[1024,256]{1,0:T(8,128)S(1)} fusion(bf16[256,256]{1,0:T(8,128)(2,1)} %get-tuple-element.229, bf16[124,256]{1,0:T(8,128)(2,1)} %get-tuple-element.228, bf16[512,124]{0,1:T(8,128)(2,1)S(1)} %get-tuple-element.195, bf16[512,124]{0,1:T(8,128)(2,1)S(1)} %get-tuple-element.196), kind=kOutput, calls=%fused_computation.1.clone.1 | convolution fusion | flops 200523776 | bytes 1497088 | tf_op jit(solution)/shard_map/while/body/eval_jaxpr/dot_general | solution.py:8
  96.8 1.6 %dynamic_update_slice.5 = f32[8,5,512]{2,0,1:T(8,128)} dynamic-update-slice(f32[8,5,512]{2,0,1:T(8,128)} %get-tuple-element.212, f32[1,5,512]{2,0,1:T(1,128)S(1)} %copy.60, s32[]{:T(128)} %get-tuple-element.211, s32[]{:T(128)} %constant.20.clone.1..sunk, s32[]{:T(128)} %constant.20.clone.1..sunk) | dynamic-update-slice | bytes 20484 | tf_op jit(solution)/shard_map/while/body/jit(dynamic_update_index_in_dim)/dynamic_update_slice | solution.py:75
  99.3 7.5 %all_to_all.21 = f32[8,5,4,128]{3,2,1,0:T(4,128)S(1)} all-to-all(f32[8,5,4,128]{3,2,1,0:T(4,128)S(1)} %copy.46), channel_id=1, replica_groups=mesh['dp'=8,'mp'=4] {'dp'}, dimensions={0} | all-to-all | bytes 163840 | tf_op jit(solution)/shard_map/all_to_all | solution.py:78
  107.4 3.3 %all-to-all-start.3 = ((f32[8,5,4,128]{3,0,1,2:T(8,128)}), f32[8,5,4,128]{3,0,1,2:T(8,128)S(1)}, u32[]{:S(2)}, u32[]{:S(2)}) async-start(f32[8,5,4,128]{3,0,1,2:T(8,128)} %copy.47), calls=%async_computation.3 | async-start | bytes 163840 | tf_op jit(solution)/shard_map/all_to_all | solution.py:77
  111.1 5.4 %all-to-all-done.3 = f32[8,5,4,128]{3,0,1,2:T(8,128)S(1)} async-done(((f32[8,5,4,128]{3,0,1,2:T(8,128)}), f32[8,5,4,128]{3,0,1,2:T(8,128)S(1)}, u32[]{:S(2)}, u32[]{:S(2)}) %all-to-all-start.3) | async-done | bytes 81952 | tf_op jit(solution)/shard_map/all_to_all | solution.py:77
  (154 shorter events, 28.6 us)
Async XLA Ops:
  0.6 24.7 %copy-start = (bf16[2048,256]{1,0:T(8,128)(2,1)S(1)}, bf16[2048,256]{1,0:T(8,128)(2,1)}, u32[]{:S(2)}) copy-start(bf16[2048,256]{1,0:T(8,128)(2,1)} %param.11) | copy-start | bytes 3145732
  2.0 2.4 %copy-start.6 = (s32[1024]{0:T(1024)}, s32[1024]{0:T(1024)S(1)}, u32[]{:S(2)}) copy-start(s32[1024]{0:T(1024)S(1)} %convert_reduce_fusion) | copy-start | bytes 12292
  14.8 10.5 %all-to-all-start.1 = ((s32[8,4,128]{2,0,1:T(8,128)}), s32[8,4,128]{2,0,1:T(8,128)S(1)}, u32[]{:S(2)}, u32[]{:S(2)}) async-start(s32[8,4,128]{2,0,1:T(8,128)} %copy.41), calls=%async_computation.1 | async-start | bytes 32768 | tf_op jit(solution)/shard_map/all_to_all | solution.py:63
  45.1 1.5 %copy-start.1 = (bf16[2,256]{1,0:T(2,128)(2,1)S(1)}, bf16[2,256]{1,0:T(2,128)(2,1)}, u32[]{:S(2)}) copy-start(bf16[2,256]{1,0:T(2,128)(2,1)} %param.16) | copy-start | bytes 3076
  46.7 64.0 %copy-start.3 = (s32[1024,1]{0,1:T(1,128)S(1)}, s32[1024,1]{0,1:T(1,128)}, u32[]{:S(2)}) copy-start(s32[1024,1]{0,1:T(1,128)} %param.12) | copy-start | bytes 12292
  46.7 69.8 %copy-start.7 = (s32[1024]{0:T(1024)S(1)}, s32[1024]{0:T(1024)}, u32[]{:S(2)}) copy-start(s32[1024]{0:T(1024)} %copy-done.6) | copy-start | bytes 12292
  46.7 2.6 %copy-start.5 = (bf16[256]{0:T(256)(128)(2,1)S(1)}, bf16[256]{0:T(256)(128)(2,1)}, u32[]{:S(2)}) copy-start(bf16[256]{0:T(256)(128)(2,1)} %get-tuple-element.230) | copy-start | bytes 1540 | tf_op jit(solution)/shard_map/while
  46.7 3.2 %copy-start.4 = (bf16[2,256,256]{2,1,0:T(8,128)(2,1)S(1)}, bf16[2,256,256]{2,1,0:T(8,128)(2,1)}, u32[]{:S(2)}) copy-start(bf16[2,256,256]{2,1,0:T(8,128)(2,1)} %get-tuple-element.226) | copy-start | bytes 786436 | tf_op jit(solution)/shard_map/while
  53.2 2.6 %copy-start.5 = (bf16[256]{0:T(256)(128)(2,1)S(1)}, bf16[256]{0:T(256)(128)(2,1)}, u32[]{:S(2)}) copy-start(bf16[256]{0:T(256)(128)(2,1)} %get-tuple-element.230) | copy-start | bytes 1540 | tf_op jit(solution)/shard_map/while
  53.2 3.2 %copy-start.4 = (bf16[2,256,256]{2,1,0:T(8,128)(2,1)S(1)}, bf16[2,256,256]{2,1,0:T(8,128)(2,1)}, u32[]{:S(2)}) copy-start(bf16[2,256,256]{2,1,0:T(8,128)(2,1)} %get-tuple-element.226) | copy-start | bytes 786436 | tf_op jit(solution)/shard_map/while
  59.6 2.6 %copy-start.5 = (bf16[256]{0:T(256)(128)(2,1)S(1)}, bf16[256]{0:T(256)(128)(2,1)}, u32[]{:S(2)}) copy-start(bf16[256]{0:T(256)(128)(2,1)} %get-tuple-element.230) | copy-start | bytes 1540 | tf_op jit(solution)/shard_map/while
  59.6 3.2 %copy-start.4 = (bf16[2,256,256]{2,1,0:T(8,128)(2,1)S(1)}, bf16[2,256,256]{2,1,0:T(8,128)(2,1)}, u32[]{:S(2)}) copy-start(bf16[2,256,256]{2,1,0:T(8,128)(2,1)} %get-tuple-element.226) | copy-start | bytes 786436 | tf_op jit(solution)/shard_map/while
  66.1 2.6 %copy-start.5 = (bf16[256]{0:T(256)(128)(2,1)S(1)}, bf16[256]{0:T(256)(128)(2,1)}, u32[]{:S(2)}) copy-start(bf16[256]{0:T(256)(128)(2,1)} %get-tuple-element.230) | copy-start | bytes 1540 | tf_op jit(solution)/shard_map/while
  66.1 3.2 %copy-start.4 = (bf16[2,256,256]{2,1,0:T(8,128)(2,1)S(1)}, bf16[2,256,256]{2,1,0:T(8,128)(2,1)}, u32[]{:S(2)}) copy-start(bf16[2,256,256]{2,1,0:T(8,128)(2,1)} %get-tuple-element.226) | copy-start | bytes 786436 | tf_op jit(solution)/shard_map/while
  72.6 2.6 %copy-start.5 = (bf16[256]{0:T(256)(128)(2,1)S(1)}, bf16[256]{0:T(256)(128)(2,1)}, u32[]{:S(2)}) copy-start(bf16[256]{0:T(256)(128)(2,1)} %get-tuple-element.230) | copy-start | bytes 1540 | tf_op jit(solution)/shard_map/while
  72.6 3.2 %copy-start.4 = (bf16[2,256,256]{2,1,0:T(8,128)(2,1)S(1)}, bf16[2,256,256]{2,1,0:T(8,128)(2,1)}, u32[]{:S(2)}) copy-start(bf16[2,256,256]{2,1,0:T(8,128)(2,1)} %get-tuple-element.226) | copy-start | bytes 786436 | tf_op jit(solution)/shard_map/while
  79.0 2.6 %copy-start.5 = (bf16[256]{0:T(256)(128)(2,1)S(1)}, bf16[256]{0:T(256)(128)(2,1)}, u32[]{:S(2)}) copy-start(bf16[256]{0:T(256)(128)(2,1)} %get-tuple-element.230) | copy-start | bytes 1540 | tf_op jit(solution)/shard_map/while
  79.0 3.2 %copy-start.4 = (bf16[2,256,256]{2,1,0:T(8,128)(2,1)S(1)}, bf16[2,256,256]{2,1,0:T(8,128)(2,1)}, u32[]{:S(2)}) copy-start(bf16[2,256,256]{2,1,0:T(8,128)(2,1)} %get-tuple-element.226) | copy-start | bytes 786436 | tf_op jit(solution)/shard_map/while
  85.5 2.6 %copy-start.5 = (bf16[256]{0:T(256)(128)(2,1)S(1)}, bf16[256]{0:T(256)(128)(2,1)}, u32[]{:S(2)}) copy-start(bf16[256]{0:T(256)(128)(2,1)} %get-tuple-element.230) | copy-start | bytes 1540 | tf_op jit(solution)/shard_map/while
  85.5 3.2 %copy-start.4 = (bf16[2,256,256]{2,1,0:T(8,128)(2,1)S(1)}, bf16[2,256,256]{2,1,0:T(8,128)(2,1)}, u32[]{:S(2)}) copy-start(bf16[2,256,256]{2,1,0:T(8,128)(2,1)} %get-tuple-element.226) | copy-start | bytes 786436 | tf_op jit(solution)/shard_map/while
  91.9 2.6 %copy-start.5 = (bf16[256]{0:T(256)(128)(2,1)S(1)}, bf16[256]{0:T(256)(128)(2,1)}, u32[]{:S(2)}) copy-start(bf16[256]{0:T(256)(128)(2,1)} %get-tuple-element.230) | copy-start | bytes 1540 | tf_op jit(solution)/shard_map/while
  91.9 3.2 %copy-start.4 = (bf16[2,256,256]{2,1,0:T(8,128)(2,1)S(1)}, bf16[2,256,256]{2,1,0:T(8,128)(2,1)}, u32[]{:S(2)}) copy-start(bf16[2,256,256]{2,1,0:T(8,128)(2,1)} %get-tuple-element.226) | copy-start | bytes 786436 | tf_op jit(solution)/shard_map/while
  107.4 9.1 %all-to-all-start.3 = ((f32[8,5,4,128]{3,0,1,2:T(8,128)}), f32[8,5,4,128]{3,0,1,2:T(8,128)S(1)}, u32[]{:S(2)}, u32[]{:S(2)}) async-start(f32[8,5,4,128]{3,0,1,2:T(8,128)} %copy.47), calls=%async_computation.3 | async-start | bytes 163840 | tf_op jit(solution)/shard_map/all_to_all | solution.py:77
  117.1 1.2 %copy-start.2 = (f32[1,1024]{1,0:T(1,128)}, f32[1,1024]{1,0:T(1,128)S(1)}, u32[]{:S(2)}) copy-start(f32[1,1024]{1,0:T(1,128)S(1)} %get-tuple-element.126) | copy-start | bytes 12292
where the time goes:
time: 120 us; the launch traced here: 118 us
  local copies, waits for them, and re-layouts  45.1 us (38%)
  matrix products  31.9 us (27%)
  blocking collectives  17.2 us (14%)
  waiting for transfers between devices  10.1 us (8%)
  starting transfers between devices  8.16 us (7%)
  other arithmetic  4.53 us (4%)
    gather x2, local copies, waits for them, and re-layouts, body(): picked = jnp.take(buffer, jnp.maximum(asked, 0).reshape(-1), axis=0)  19.8 us
    dot_general x24, matrix products, layer_two(): jnp.dot(first, mid, preferred_element_type=jnp.float32)  19.4 us
    dynamic_update_slice x16, local copies, waits for them, and re-layouts, body(): lax.map(evaluate, picked.reshape(outer, inner * slots_each, columns_all))  12.5 us
    dot_general x24, matrix products, layer_two(): jnp.dot(hidden, out.astype(jnp.float32), precision=lax.Precision.HIGHEST)  10.2 us
    all_to_all x1, blocking collectives, body(): lax.all_to_all(requests, 'dp', split_axis=0, concat_axis=0, tiled=True)  9.75 us
    squeeze x8, local copies, waits for them, and re-layouts, body(): lax.map(evaluate, picked.reshape(outer, inner * slots_each, columns_all))  8.09 us
    all_to_all x1, blocking collectives, body(): lax.all_to_all(served, 'dp', split_axis=0, concat_axis=0, tiled=True)  7.49 us
    all_to_all x1, waiting for transfers between devices, body(): lax.all_to_all(lax.all_to_all(served, 'dp', split_axis=0, concat_axis=0,...  5.37 us
  transfers between devices with their start and end apart: 2, of which 2 were waited for; matrix products, arithmetic and copies ran while one was open for 1% of the time, Pallas kernels for 0%

commit v1 on v0

v1 whole, which is shorter than its diff:
```python
import functools

import jax
import jax.numpy as jnp
from jax import lax
from jax.experimental import pallas as pl
from jax.experimental.pallas import tpu as pltpu
from jax.sharding import PartitionSpec as P

MESH = pl.DeviceIdType.MESH
PARTS = 4
LANES = 256
KINDS = 8


def log2(value):
    bits = value.bit_length() - 1
    assert 1 << bits == value
    return bits


def orders_of(dp_size, mp_size):
    mp_bits, dp_bits = log2(mp_size), log2(dp_size)
    last = mp_bits
    first = mp_bits - 1
    others = [b for b in range(mp_bits + dp_bits) if b not in (last, first)]
    orders = []
    for part in range(PARTS):
        turn = part % len(others)
        orders.append([first] + others[turn:] + others[:turn] + [last])
    return orders


def kernel(
    dp_size,
    mp_size,
    buffer,
    owner_ref,
    row_ref,
    q_in_ref,
    q_mid_ref,
    q_out_ref,
    v_in_ref,
    v_mid_ref,
    v_out_ref,
    q_values_ref,
    values_ref,
    targets_ref,
    q_loss_ref,
    value_loss_ref,
    rows_v,
    wide,
    first_w,
    mid_w,
    out_w,
    table,
    hot,
    place,
    load_sem,
    send_sem,
    recv_sem,
    pass_send_sem,
    pass_recv_sem,
):
    f32, bf16 = jnp.float32, jnp.bfloat16
    orders = orders_of(dp_size, mp_size)
    mp_bits = log2(mp_size)
    steps = len(orders[0]) - 1
    half = 1 << steps
    dp, mp = lax.axis_index("dp"), lax.axis_index("mp")
    me = dp * mp_size + mp
    rows_dev = buffer.shape[0]
    part_rows = rows_dev // PARTS
    groups = part_rows // LANES
    states_width = v_in_ref.shape[0]
    pair_width = q_in_ref.shape[1]
    hidden = v_mid_ref.shape[0]
    batch = row_ref.shape[1]

    def load(part):
        span = pl.ds(part * part_rows, part_rows)
        return pltpu.make_async_copy(buffer.at[span], rows_v.at[span], load_sem.at[part])

    for part in range(PARTS):
        load(part).start()

    def partner(bit):
        if bit < mp_bits:
            step = 1 << bit
            return (dp, mp + step * (1 - 2 * ((mp // step) % 2)))
        step = 1 << (bit - mp_bits)
        return (dp + step * (1 - 2 * ((dp // step) % 2)), mp)

    barrier = pltpu.get_barrier_semaphore()
    for bit in sorted(orders[0]):
        pl.semaphore_signal(barrier, inc=1, device_id=partner(bit), device_id_type=MESH)

    def padded(value):
        wide[...] = jnp.zeros_like(wide)
        wide[0 : value.shape[0], :] = value.astype(f32)
        return wide[...].T

    for head in range(2):
        first_w[head * hidden : (head + 1) * hidden, :] = padded(q_in_ref[head]).astype(bf16)
        mid_w[head] = q_mid_ref[head].astype(f32).T.astype(bf16)
    value_w = padded(v_in_ref[...])
    first_w[2 * hidden : 3 * hidden, :] = value_w.astype(bf16)
    first_w[3 * hidden : 4 * hidden, :] = pltpu.roll(value_w, pair_width, 1).astype(bf16)
    mid_w[2] = v_mid_ref[...].astype(f32).T.astype(bf16)
    unit = lax.broadcasted_iota(jnp.int32, (16, LANES), 1)
    pick = lax.broadcasted_iota(jnp.int32, (16, LANES), 0)
    first_w[4 * hidden : 4 * hidden + 16, :] = jnp.where(
        (unit == pick + (pair_width + states_width)) & (pick < 2), 1.0, 0.0
    ).astype(bf16)
    wide[0:2, :] = q_out_ref[...].astype(f32)
    wide[2:3, :] = v_out_ref[...].astype(f32)
    columns = wide[0:8, :].T
    for head in range(3):
        out_w[head] = jnp.broadcast_to(columns[:, head : head + 1], (hidden, 128))

    wanted = row_ref[...]
    relative = owner_ref[...] ^ me
    low = wanted & (LANES - 1)
    group = wanted // LANES
    hot[...] = jnp.where(
        lax.broadcasted_iota(jnp.int32, (LANES, batch), 0) == low, 1.0, 0.0
    ).astype(bf16)
    for part in range(PARTS):
        slot = jnp.zeros_like(relative)
        for position, bit in enumerate(orders[part]):
            slot = slot + (((relative >> bit) & 1) << position)
        here = (group // groups) == part
        index = jnp.where(here, slot * groups + (group - part * groups), -1)
        place[part] = jnp.broadcast_to(index, (KINDS, batch))

    def send(part, step):
        count = 1 << step
        return pltpu.make_async_remote_copy(
            src_ref=table.at[part, pl.ds(0, count)],
            dst_ref=table.at[part, pl.ds(count, count)],
            send_sem=send_sem.at[part, step],
            recv_sem=recv_sem.at[part, step],
            device_id=partner(orders[part][step]),
            device_id_type=MESH,
        )

    def span_of(stage):
        return (0, 1) if stage == 0 else (1 << (stage - 1), 1 << (stage - 1))

    def hand_over(part, stage):
        start, count = span_of(stage)
        return pltpu.make_async_remote_copy(
            src_ref=table.at[part, pl.ds(start, count)],
            dst_ref=table.at[part, pl.ds(half + start, count)],
            send_sem=pass_send_sem.at[part, stage],
            recv_sem=pass_recv_sem.at[part, stage],
            device_id=partner(orders[part][-1]),
            device_id_type=MESH,
        )

    def evaluate(part):
        blocks = []
        for g in range(groups):
            start = part * part_rows + g * LANES
            block = rows_v[start : start + LANES, :]
            ones = lax.dot_general(
                first_w[...], block, (((1,), (1,)), ((), ())), preferred_element_type=f32
            )
            outs = []
            for head in range(4):
                h1 = jnp.maximum(ones[head * hidden : (head + 1) * hidden], 0.0).astype(bf16)
                kind = min(head, 2)
                h2 = jnp.maximum(
                    jnp.dot(mid_w[kind], h1, preferred_element_type=f32), 0.0
                )
                weight = out_w[kind]
                outs.append(
                    jnp.concatenate(
                        [
                            jnp.sum(h2[:, n : n + 128] * weight, axis=0, keepdims=True)
                            for n in range(0, LANES, 128)
                        ],
                        axis=1,
                    )
                )
            reward = ones[4 * hidden : 4 * hidden + 1]
            discount = ones[4 * hidden + 1 : 4 * hidden + 2]
            q_first, q_second, value_now, value_next = outs
            targets = reward + discount * value_next
            q_loss = (q_first - targets) ** 2 + (q_second - targets) ** 2
            gap = jnp.minimum(q_first, q_second) - value_now
            value_loss = jnp.where(gap < 0.0, 0.3, 0.7) * gap * gap
            blocks += [
                q_first,
                q_second,
                value_now,
                value_next,
                targets,
                q_loss,
                value_loss,
                jnp.zeros_like(q_loss),
            ]
        table[part, 0] = jnp.concatenate(blocks, axis=0).astype(bf16)

    def select(acc, part, start, count):
        def some(acc, start, count):
            piece = table[part, pl.ds(start, count)].reshape(count * groups * KINDS, LANES)
            found = jnp.dot(piece, hot[...], preferred_element_type=f32)
            where = place[part]
            for j in range(count * groups):
                acc = jnp.where(
                    where == start * groups + j, found[j * KINDS : (j + 1) * KINDS], acc
                )
            return acc

        if count <= 8:
            return some(acc, start, count)
        return lax.fori_loop(0, count // 8, lambda i, a: some(a, start + i * 8, 8), acc)

    acc = jnp.zeros((KINDS, batch), f32)

    def arrived(part, step):
        send(part, step).wait_recv()
        if step + 1 < steps:
            send(part, step + 1).start()
        hand_over(part, step + 1).start()

    events = sorted(
        ((part * 0.8 + step * 1.8, part, step) for part in range(PARTS) for step in range(steps)),
    )
    pending = list(events)
    for part in range(PARTS):
        load(part).wait()
        evaluate(part)
        if part == 0:
            pl.semaphore_wait(barrier, len(orders[0]))
        send(part, 0).start()
        hand_over(part, 0).start()
        if part >= 2:
            _, p, s = pending.pop(0)
            arrived(p, s)
    for part in range(PARTS):
        acc = select(acc, part, 0, 1)
    for part in range(PARTS):
        hand_over(part, 0).wait_recv()
        acc = select(acc, part, half, 1)
    done = [(p, s) for (_, p, s) in events if not any(q[1:] == (p, s) for q in pending)]
    late = []
    for p, s in done:
        start, count = span_of(s + 1)
        acc = select(acc, p, start, count)
        late.append((p, s))
    for _, p, s in pending:
        arrived(p, s)
        start, count = span_of(s + 1)
        acc = select(acc, p, start, count)
        late.append((p, s))
        if len(late) > 3:
            p, s = late.pop(0)
            hand_over(p, s + 1).wait_recv()
            start, count = span_of(s + 1)
            acc = select(acc, p, half + start, count)
    for p, s in late:
        hand_over(p, s + 1).wait_recv()
        start, count = span_of(s + 1)
        acc = select(acc, p, half + start, count)
    q_values_ref[...] = acc[0:2]
    values_ref[...] = acc[2:4]
    targets_ref[...] = acc[4:5]
    q_loss_ref[...] = acc[5:6]
    value_loss_ref[...] = acc[6:7]
    for part in range(PARTS):
        for step in range(steps):
            send(part, step).wait_send()
        for stage in range(steps + 1):
            hand_over(part, stage).wait_send()


def body(buffer, owner, local_row, q_in, q_mid, q_out, v_in, v_mid, v_out):
    dp_size, mp_size = lax.axis_size("dp"), lax.axis_size("mp")
    owners = dp_size * mp_size
    batch = local_row.shape[0]
    rows_dev, width = buffer.shape
    hidden = v_mid.shape[0]
    assert width == LANES and hidden == LANES
    groups = rows_dev // PARTS // LANES
    steps = log2(owners) - 1
    f32, bf16 = jnp.float32, jnp.bfloat16
    vmem = pl.BlockSpec(memory_space=pltpu.VMEM)
    outs = pl.pallas_call(
        functools.partial(kernel, dp_size, mp_size),
        out_shape=(
            jax.ShapeDtypeStruct((2, batch), f32),
            jax.ShapeDtypeStruct((2, batch), f32),
            jax.ShapeDtypeStruct((1, batch), f32),
            jax.ShapeDtypeStruct((1, batch), f32),
            jax.ShapeDtypeStruct((1, batch), f32),
        ),
        in_specs=[pl.BlockSpec(memory_space=pl.ANY)] + [vmem] * 8,
        out_specs=(vmem,) * 5,
        scratch_shapes=[
            pltpu.VMEM((rows_dev, width), bf16),
            pltpu.VMEM((width, hidden), f32),
            pltpu.VMEM((4 * hidden + 16, width), bf16),
            pltpu.VMEM((3, hidden, hidden), bf16),
            pltpu.VMEM((3, hidden, 128), f32),
            pltpu.VMEM((PARTS, owners, groups * KINDS, LANES), bf16),
            pltpu.VMEM((LANES, batch), bf16),
            pltpu.VMEM((PARTS, KINDS, batch), jnp.int32),
            pltpu.SemaphoreType.DMA((PARTS,)),
            pltpu.SemaphoreType.DMA((PARTS, steps)),
            pltpu.SemaphoreType.DMA((PARTS, steps)),
            pltpu.SemaphoreType.DMA((PARTS, steps + 1)),
            pltpu.SemaphoreType.DMA((PARTS, steps + 1)),
        ],
        compiler_params=pltpu.CompilerParams(
            collective_id=0, has_side_effects=True, vmem_limit_bytes=48 << 20
        ),
        name="critic_exchange",
    )(
        buffer,
        owner.reshape(1, batch),
        local_row.reshape(1, batch),
        q_in,
        q_mid,
        q_out,
        v_in,
        v_mid,
        v_out.reshape(1, hidden),
    )
    q_values, values, targets, q_loss, value_loss = outs
    return (
        q_values,
        values,
        targets.reshape(batch),
        q_loss.reshape(batch),
        value_loss.reshape(batch),
    )


def solution(mesh):
    return jax.shard_map(
        body,
        mesh=mesh,
        in_specs=(
            P(("dp", "mp"), None),
            P(("dp", "mp"), None),
            P(("dp", "mp")),
            P(),
            P(),
            P(),
            P(),
            P(),
            P(),
        ),
        out_specs=(
            P(None, ("dp", "mp")),
            P(None, ("dp", "mp")),
            P(("dp", "mp")),
            P(("dp", "mp")),
            P(("dp", "mp")),
        ),
        check_vma=False,
    )
```

time: 120 us -> 32.2 us (0.27); the launches traced: 118 us -> 31.9 us
  local copies, waits for them, and re-layouts: 45.1 us -> 7.62 us
  matrix products: 31.9 us -> 0 us
  Pallas kernels: 0 us -> 23.6 us
  blocking collectives: 17.2 us -> 0 us
  waiting for transfers between devices: 10.1 us -> 0 us
  starting transfers between devices: 8.16 us -> 0 us
  other arithmetic: 4.53 us -> 0 us
    dot_general x50 -> x0, matrix products: 31.9 us -> none  [the longest x24 19.4 us: layer_two(): jnp.dot(first, mid, preferred_element_type=jnp.float32)]
    pallas_call x0 -> x1, Pallas kernels: none -> 23.6 us  [body(): pl.pallas_call(functools.partial(kernel, dp_size, mp_size), out_shape=(ja...]
    gather x2 -> x0, local copies, waits for them, and re-layouts: 19.8 us -> none  [body(): picked = jnp.take(buffer, jnp.maximum(asked, 0).reshape(-1), axis=0)]
    all_to_all x2 -> x0, blocking collectives: 17.2 us -> none  [the longest x1 9.75 us: body(): lax.all_to_all(requests, 'dp', split_axis=0, concat_axis=0, tiled=True)]
    dynamic_update_slice x16 -> x0, local copies, waits for them, and re-layouts: 12.5 us -> none  [body(): lax.map(evaluate, picked.reshape(outer, inner * slots_each, columns_all))]
    all_to_all x2 -> x0, waiting for transfers between devices: 10.1 us -> none  [the longest x1 5.37 us: body(): lax.all_to_all(lax.all_to_all(served, 'dp', split_axis=0, concat_axis=0,...]
    all_to_all x2 -> x0, starting transfers between devices: 8.16 us -> none  [the longest x1 4.87 us: body(): lax.all_to_all(lax.all_to_all(requests, 'dp', split_axis=0, concat_axis=0...]
    squeeze x8 -> x0, local copies, waits for them, and re-layouts: 8.09 us -> none  [body(): lax.map(evaluate, picked.reshape(outer, inner * slots_each, columns_all))]
  transfers between devices with their start and end apart: 2 -> 0, of which waited for: 2 -> 0; matrix products, arithmetic and copies ran while one was open for 1% -> 0% of each run, Pallas kernels for 0% -> 0%
where the time goes in v1:
time: 32.2 us; the launch traced here: 31.9 us
  Pallas kernels  23.6 us (73%)
  local copies, waits for them, and re-layouts  7.62 us (24%)
  between operations  0.7 us (2%)
    pallas_call x1, Pallas kernels, body(): pl.pallas_call(functools.partial(kernel, dp_size, mp_size), out_shape=(ja...  23.6 us
    unnamed x20, local copies, waits for them, and re-layouts  6.92 us
    reshape x1, local copies, waits for them, and re-layouts, body(): v_out.reshape(1, hidden)  0.7 us

profile of v1, /device:TPU:0, one launch (start us, length us, event | category | flops | bytes accessed | tf_op | source)
XLA Modules:
  0.0 31.9 jit_solution(5033877400165083584)
XLA Ops:
  0.6 0.0 copy-start.1
  0.6 0.7 %reshape.30.v_out_ref = bf16[1,256]{1,0:T(2,128)(2,1)S(1)} reshape(bf16[256]{0:T(256)(128)(2,1)} %param.17) | data formatting | bytes 1024 | tf_op jit(solution)/shard_map/reshape | solution.py:329
  1.3 0.0 copy-start.4
  1.3 0.0 copy-start.5
  1.3 0.0 copy-start.6
  1.3 1.0 %copy.14.q_in_ref = bf16[2,130,256]{2,1,0:T(8,128)(2,1)S(1)} copy(bf16[2,130,256]{2,0,1:T(2,128)(2,1)} %param.12) | data formatting | bytes 266240 | tf_op args[3]
  2.3 0.0 copy-done.1
  2.3 0.0 copy-done.4
  2.3 0.0 copy-done.5
  2.3 0.0 copy-done.6
  2.4 0.0 copy-start
  2.4 1.2 %copy-done = bf16[2048,256]{1,0:T(8,128)(2,1)S(1)} copy-done((bf16[2048,256]{1,0:T(8,128)(2,1)S(1)}, bf16[2048,256]{1,0:T(8,128)(2,1)}, u32[]{:S(2)}) %copy-start) | copy-done | bytes 1048600
  3.6 0.0 copy-start.2
  3.6 0.9 %copy-done.2 = bf16[256,256]{1,0:T(8,128)(2,1)S(1)} copy-done((bf16[256,256]{1,0:T(8,128)(2,1)S(1)}, bf16[256,256]{1,0:T(8,128)(2,1)}, u32[]{:S(2)}) %copy-start.2) | copy-done | bytes 131096
  4.5 0.0 copy-start.3
  4.5 0.8 %copy-done.3 = bf16[124,256]{1,0:T(8,128)(2,1)S(1)} copy-done((bf16[124,256]{1,0:T(8,128)(2,1)S(1)}, bf16[124,256]{1,0:T(8,128)(2,1)}, u32[]{:S(2)}) %copy-start.3) | copy-done | bytes 63512
  5.3 23.6 %critic_exchange.1 = (f32[2,1024]{1,0:T(2,128)S(1)}, f32[2,1024]{1,0:T(2,128)S(1)}, f32[1,1024]{1,0:T(1,128)S(1)}, f32[1,1024]{1,0:T(1,128)S(1)}, f32[1,1024]{1,0:T(1,128)S(1)}) custom-call(bf16[2048,256]{1,0:T(8,128)(2,1)S(1)} %copy-done, s32[1,1024]{1,0:T(1,128)S(1)} %bitcast.5, s32[1,1024]{1,0:T(1,128)S(1)} %bitcast.6, ...), custom_call_target="tpu_custom_call" | custom-call | tf_op jit(solution)/shard_map/critic_exchange/pallas_call | solution.py:290
  28.9 0.6 %copy.20 = f32[2,1024]{1,0:T(2,128)} copy(f32[2,1024]{1,0:T(2,128)S(1)} %get-tuple-element.20) | data formatting | bytes 16384
  29.5 0.6 %copy.21 = f32[2,1024]{1,0:T(2,128)} copy(f32[2,1024]{1,0:T(2,128)S(1)} %get-tuple-element.21) | data formatting | bytes 16384
  30.1 0.6 %copy.22 = f32[1024]{0:T(1024)} copy(f32[1024]{0:T(1024)S(1)} %bitcast.9) | data formatting | bytes 8192
  30.7 0.6 %copy.23 = f32[1024]{0:T(1024)} copy(f32[1024]{0:T(1024)S(1)} %bitcast.8) | data formatting | bytes 8192
  31.3 0.6 %copy.24 = f32[1024]{0:T(1024)} copy(f32[1024]{0:T(1024)S(1)} %bitcast.7) | data formatting | bytes 8192
Async XLA Ops:
  0.6 1.7 %copy-start.1 = (bf16[2,256,256]{2,1,0:T(8,128)(2,1)S(1)}, bf16[2,256,256]{2,1,0:T(8,128)(2,1)}, u32[]{:S(2)}) copy-start(bf16[2,256,256]{2,1,0:T(8,128)(2,1)} %q_mid_ref.1) | copy-start | bytes 786436
  1.3 1.0 %copy-start.4 = (s32[1024,1]{0,1:T(1,128)S(1)}, s32[1024,1]{0,1:T(1,128)}, u32[]{:S(2)}) copy-start(s32[1024,1]{0,1:T(1,128)} %param.10) | copy-start | bytes 12292
  1.3 1.0 %copy-start.5 = (s32[1024]{0:T(1024)S(1)}, s32[1024]{0:T(1024)}, u32[]{:S(2)}) copy-start(s32[1024]{0:T(1024)} %param.11) | copy-start | bytes 12292
  1.3 1.0 %copy-start.6 = (bf16[2,256]{1,0:T(2,128)(2,1)S(1)}, bf16[2,256]{1,0:T(2,128)(2,1)}, u32[]{:S(2)}) copy-start(bf16[2,256]{1,0:T(2,128)(2,1)} %q_out_ref.1) | copy-start | bytes 3076
  2.4 1.2 %copy-start = (bf16[2048,256]{1,0:T(8,128)(2,1)S(1)}, bf16[2048,256]{1,0:T(8,128)(2,1)}, u32[]{:S(2)}) copy-start(bf16[2048,256]{1,0:T(8,128)(2,1)} %buffer.1) | copy-start | bytes 3145732
  3.6 0.9 %copy-start.2 = (bf16[256,256]{1,0:T(8,128)(2,1)S(1)}, bf16[256,256]{1,0:T(8,128)(2,1)}, u32[]{:S(2)}) copy-start(bf16[256,256]{1,0:T(8,128)(2,1)} %v_mid_ref.1) | copy-start | bytes 393220
  4.5 0.8 %copy-start.3 = (bf16[124,256]{1,0:T(8,128)(2,1)S(1)}, bf16[124,256]{1,0:T(8,128)(2,1)}, u32[]{:S(2)}) copy-start(bf16[124,256]{1,0:T(8,128)(2,1)} %v_in_ref.1) | copy-start | bytes 190468

commit v2 on v1

--- a/solution.py
+++ b/solution.py
@@ -35,6 +35,15 @@
     dp_size,
     mp_size,
     buffer,
+    owner_hbm,
+    row_hbm,
+    q_in_hbm,
+    q_mid_hbm,
+    q_out_hbm,
+    v_in_hbm,
+    v_mid_hbm,
+    v_out_hbm,
+    result_ref,
     owner_ref,
     row_ref,
     q_in_ref,
@@ -43,11 +52,6 @@
     v_in_ref,
     v_mid_ref,
     v_out_ref,
-    q_values_ref,
-    values_ref,
-    targets_ref,
-    q_loss_ref,
-    value_loss_ref,
     rows_v,
     wide,
     first_w,
@@ -57,6 +61,7 @@
     hot,
     place,
     load_sem,
+    fetch_sem,
     send_sem,
     recv_sem,
     pass_send_sem,
@@ -73,7 +78,7 @@
     part_rows = rows_dev // PARTS
     groups = part_rows // LANES
     states_width = v_in_ref.shape[0]
-    pair_width = q_in_ref.shape[1]
+    pair_width = q_in_ref.shape[0]
     hidden = v_mid_ref.shape[0]
     batch = row_ref.shape[1]
 
@@ -81,6 +86,23 @@
         span = pl.ds(part * part_rows, part_rows)
         return pltpu.make_async_copy(buffer.at[span], rows_v.at[span], load_sem.at[part])
 
+    fetches = [
+        pltpu.make_async_copy(source, target, fetch_sem.at[number])
+        for number, (source, target) in enumerate(
+            (
+                (q_in_hbm, q_in_ref),
+                (v_in_hbm, v_in_ref),
+                (q_mid_hbm, q_mid_ref),
+                (v_mid_hbm, v_mid_ref),
+                (q_out_hbm, q_out_ref),
+                (v_out_hbm, v_out_ref),
+                (owner_hbm, owner_ref),
+                (row_hbm, row_ref),
+            )
+        )
+    ]
+    for fetch in fetches:
+        fetch.start()
     for part in range(PARTS):
         load(part).start()
 
@@ -100,8 +122,10 @@
         wide[0 : value.shape[0], :] = value.astype(f32)
         return wide[...].T
 
+    for fetch in fetches:
+        fetch.wait()
     for head in range(2):
-        first_w[head * hidden : (head + 1) * hidden, :] = padded(q_in_ref[head]).astype(bf16)
+        first_w[head * hidden : (head + 1) * hidden, :] = padded(q_in_ref[:, head, :]).astype(bf16)
         mid_w[head] = q_mid_ref[head].astype(f32).T.astype(bf16)
     value_w = padded(v_in_ref[...])
     first_w[2 * hidden : 3 * hidden, :] = value_w.astype(bf16)
@@ -113,7 +137,7 @@
         (unit == pick + (pair_width + states_width)) & (pick < 2), 1.0, 0.0
     ).astype(bf16)
     wide[0:2, :] = q_out_ref[...].astype(f32)
-    wide[2:3, :] = v_out_ref[...].astype(f32)
+    wide[2:3, :] = v_out_ref[...].astype(f32).reshape(1, hidden)
     columns = wide[0:8, :].T
     for head in range(3):
         out_w[head] = jnp.broadcast_to(columns[:, head : head + 1], (hidden, 128))
@@ -264,16 +288,20 @@
         hand_over(p, s + 1).wait_recv()
         start, count = span_of(s + 1)
         acc = select(acc, p, half + start, count)
-    q_values_ref[...] = acc[0:2]
-    values_ref[...] = acc[2:4]
-    targets_ref[...] = acc[4:5]
-    q_loss_ref[...] = acc[5:6]
-    value_loss_ref[...] = acc[6:7]
+    result_ref[...] = acc
     for part in range(PARTS):
         for step in range(steps):
             send(part, step).wait_send()
         for stage in range(steps + 1):
             hand_over(part, stage).wait_send()
+
+
+def spread(result_ref, q_values_ref, values_ref, targets_ref, q_loss_ref, value_loss_ref):
+    q_values_ref[...] = result_ref[0:2]
+    values_ref[...] = result_ref[2:4]
+    targets_ref[...] = result_ref[4:5]
+    q_loss_ref[...] = result_ref[5:6]
+    value_loss_ref[...] = result_ref[6:7]
 
 
 def body(buffer, owner, local_row, q_in, q_mid, q_out, v_in, v_mid, v_out):
@@ -287,18 +315,21 @@
     steps = log2(owners) - 1
     f32, bf16 = jnp.float32, jnp.bfloat16
     vmem = pl.BlockSpec(memory_space=pltpu.VMEM)
-    outs = pl.pallas_call(
+    hbm = pl.BlockSpec(memory_space=pltpu.HBM)
+    result = pl.pallas_call(
         functools.partial(kernel, dp_size, mp_size),
-        out_shape=(
-            jax.ShapeDtypeStruct((2, batch), f32),
-            jax.ShapeDtypeStruct((2, batch), f32),
-            jax.ShapeDtypeStruct((1, batch), f32),
-            jax.ShapeDtypeStruct((1, batch), f32),
-            jax.ShapeDtypeStruct((1, batch), f32),
-        ),
-        in_specs=[pl.BlockSpec(memory_space=pl.ANY)] + [vmem] * 8,
-        out_specs=(vmem,) * 5,
+        out_shape=pltpu.VMEM((KINDS, batch), f32),
+        in_specs=[hbm] * 9,
+        out_specs=vmem,
         scratch_shapes=[
+            pltpu.VMEM((1, batch), jnp.int32),
+            pltpu.VMEM((1, batch), jnp.int32),
+            pltpu.VMEM((q_in.shape[1], 2, hidden), bf16),
+            pltpu.VMEM(q_mid.shape, bf16),
+            pltpu.VMEM(q_out.shape, bf16),
+            pltpu.VMEM(v_in.shape, bf16),
+            pltpu.VMEM(v_mid.shape, bf16),
+            pltpu.VMEM(v_out.shape, bf16),
             pltpu.VMEM((rows_dev, width), bf16),
             pltpu.VMEM((width, hidden), f32),
             pltpu.VMEM((4 * hidden + 16, width), bf16),
@@ -308,6 +339,7 @@
             pltpu.VMEM((LANES, batch), bf16),
             pltpu.VMEM((PARTS, KINDS, batch), jnp.int32),
             pltpu.SemaphoreType.DMA((PARTS,)),
+            pltpu.SemaphoreType.DMA((8,)),
             pltpu.SemaphoreType.DMA((PARTS, steps)),
             pltpu.SemaphoreType.DMA((PARTS, steps)),
             pltpu.SemaphoreType.DMA((PARTS, steps + 1)),
@@ -318,16 +350,31 @@
         ),
         name="critic_exchange",
     )(
-        buffer,
-        owner.reshape(1, batch),
-        local_row.reshape(1, batch),
-        q_in,
-        q_mid,
-        q_out,
-        v_in,
-        v_mid,
-        v_out.reshape(1, hidden),
+        *(
+            pltpu.with_memory_space_constraint(x, pltpu.HBM)
+            for x in (
+                buffer,
+                owner.reshape(1, batch),
+                local_row.reshape(1, batch),
+                jnp.transpose(q_in, (1, 0, 2)),
+                q_mid,
+                q_out,
+                v_in,
+                v_mid,
+                v_out,
+            )
+        )
     )
+    one = jax.ShapeDtypeStruct((1, batch), f32)
+    two = jax.ShapeDtypeStruct((2, batch), f32)
+    outs = pl.pallas_call(
+        spread,
+        out_shape=(two, two, one, one, one),
+        in_specs=[vmem],
+        out_specs=(vmem,) * 5,
+        compiler_params=pltpu.CompilerParams(vmem_limit_bytes=1 << 20),
+        name="spread",
+    )(result)
     q_values, values, targets, q_loss, value_loss = outs
     return (
         q_values,

time: 32.2 us -> 25.9 us (0.80)
  local copies, waits for them, and re-layouts: 7.62 us -> 0 us
  Pallas kernels: 23.6 us -> 25.1 us
    unnamed x20 -> x0, local copies, waits for them, and re-layouts: 6.92 us -> none
    pallas_call x1 -> x2, Pallas kernels: 23.6 us -> 25.1 us  [the longest x1 24.5 us: body(): pl.pallas_call(functools.partial(kernel, dp_size, mp_size), out_shape=plt...]
    reshape x1 -> x0, local copies, waits for them, and re-layouts: 0.7 us -> none  [body(): v_out.reshape(1, hidden)]
where the time goes in v2:
time: 25.9 us; the launch traced here: 25.8 us
  Pallas kernels  25.1 us (97%)
  between operations  0.64 us (2%)
    pallas_call x1, Pallas kernels, body(): pl.pallas_call(functools.partial(kernel, dp_size, mp_size), out_shape=plt...  24.5 us
    pallas_call x1, Pallas kernels, body(): pl.pallas_call(spread, out_shape=(two, two, one, one, one), in_specs=[vme...  0.62 us

profile of v2, /device:TPU:0, one launch (start us, length us, event | category | flops | bytes accessed | tf_op | source)
XLA Modules:
  0.0 25.8 jit_solution(14082191816177108760)
XLA Ops:
  0.6 24.5 %critic_exchange.1.result_ref = f32[8,1024]{1,0:T(8,128)S(1)} custom-call(bf16[2048,256]{1,0:T(8,128)(2,1)} %buffer.1, s32[1,1024]{1,0:T(1,128)} %bitcast.7, s32[1,1024]{1,0:T(1,128)} %bitcast.8, bf16[130,2,256]{2,1,0:T(2,128)(2,1)} %bitcast.6, bf16[2,256,256]{2,1,0:T(8,128)(2,1)} %q_mid_hbm.1, bf16[2,256]{1,0:T(2,128)(2,1)} %q_out_hbm.1, ...), custom_call_target="tpu_custom_call" | custom-call | tf_op jit(solution)/shard_map/critic_exchange/pallas_call | solution.py:319
  25.1 0.6 %spread.1 = (f32[2,1024]{1,0:T(2,128)}, f32[2,1024]{1,0:T(2,128)}, f32[1,1024]{1,0:T(1,128)}, f32[1,1024]{1,0:T(1,128)}, f32[1,1024]{1,0:T(1,128)}) custom-call(f32[8,1024]{1,0:T(8,128)S(1)} %critic_exchange.1.result_ref), custom_call_target="tpu_custom_call" | custom-call | tf_op jit(solution)/shard_map/spread/pallas_call | solution.py:370

commit v3 on v2

--- a/solution.py
+++ b/solution.py
@@ -8,9 +8,10 @@
 from jax.sharding import PartitionSpec as P
 
 MESH = pl.DeviceIdType.MESH
-PARTS = 4
+PARTS = 2
 LANES = 256
 KINDS = 8
+EVERY, STAGE, HOP, BEHIND = 0.9, 2.4, 0.8, 6
 
 
 def log2(value):
@@ -19,16 +20,24 @@
     return bits
 
 
-def orders_of(dp_size, mp_size):
+def plan_of(dp_size, mp_size):
     mp_bits, dp_bits = log2(mp_size), log2(dp_size)
     last = mp_bits
-    first = mp_bits - 1
-    others = [b for b in range(mp_bits + dp_bits) if b not in (last, first)]
-    orders = []
-    for part in range(PARTS):
-        turn = part % len(others)
-        orders.append([first] + others[turn:] + others[:turn] + [last])
-    return orders
+    inner = list(range(mp_bits))
+    outer = [b for b in range(mp_bits, mp_bits + dp_bits) if b != last]
+    stages = [bits[n : n + 2] for bits in (inner, outer) for n in range(0, len(bits), 2)]
+    return [(stages, last) for _ in range(PARTS)]
+
+
+def pieces_of(stages):
+    pieces, count = [], 1
+    for number, bits in enumerate(stages):
+        combos = range(1, 1 << len(bits))
+        for combo in sorted(combos, key=lambda c: (c.bit_count(), c)):
+            mask = sum(1 << b for n, b in enumerate(bits) if (combo >> n) & 1)
+            pieces.append((number, mask, combo * count, count))
+        count <<= len(bits)
+    return pieces, count
 
 
 def kernel(
@@ -68,10 +77,10 @@
     pass_recv_sem,
 ):
     f32, bf16 = jnp.float32, jnp.bfloat16
-    orders = orders_of(dp_size, mp_size)
+    plan = plan_of(dp_size, mp_size)
     mp_bits = log2(mp_size)
-    steps = len(orders[0]) - 1
-    half = 1 << steps
+    pieces = [pieces_of(stages)[0] for stages, _ in plan]
+    half = pieces_of(plan[0][0])[1]
     dp, mp = lax.axis_index("dp"), lax.axis_index("mp")
     me = dp * mp_size + mp
     rows_dev = buffer.shape[0]
@@ -106,16 +115,19 @@
     for part in range(PARTS):
         load(part).start()
 
-    def partner(bit):
-        if bit < mp_bits:
-            step = 1 << bit
-            return (dp, mp + step * (1 - 2 * ((mp // step) % 2)))
-        step = 1 << (bit - mp_bits)
-        return (dp + step * (1 - 2 * ((dp // step) % 2)), mp)
-
+    def partner(mask):
+        there = [mp, dp]
+        for bit in range(mask.bit_length()):
+            if (mask >> bit) & 1:
+                axis, step = (0, 1 << bit) if bit < mp_bits else (1, 1 << (bit - mp_bits))
+                there[axis] = there[axis] + step * (1 - 2 * ((there[axis] // step) % 2))
+        return (there[1], there[0])
+
+    partners = {mask for sends in pieces for _, mask, _, _ in sends}
+    partners |= {1 << last for _, last in plan if last is not None}
     barrier = pltpu.get_barrier_semaphore()
-    for bit in sorted(orders[0]):
-        pl.semaphore_signal(barrier, inc=1, device_id=partner(bit), device_id_type=MESH)
+    for mask in sorted(partners):
+        pl.semaphore_signal(barrier, inc=1, device_id=partner(mask), device_id_type=MESH)
 
     def padded(value):
         wide[...] = jnp.zeros_like(wide)
@@ -151,34 +163,33 @@
     ).astype(bf16)
     for part in range(PARTS):
         slot = jnp.zeros_like(relative)
-        for position, bit in enumerate(orders[part]):
+        stages, last = plan[part]
+        bits = [bit for stage in stages for bit in stage]
+        for position, bit in enumerate(bits + ([] if last is None else [last])):
             slot = slot + (((relative >> bit) & 1) << position)
         here = (group // groups) == part
         index = jnp.where(here, slot * groups + (group - part * groups), -1)
         place[part] = jnp.broadcast_to(index, (KINDS, batch))
 
-    def send(part, step):
-        count = 1 << step
+    def send(part, number):
+        _, mask, start, count = pieces[part][number]
         return pltpu.make_async_remote_copy(
             src_ref=table.at[part, pl.ds(0, count)],
-            dst_ref=table.at[part, pl.ds(count, count)],
-            send_sem=send_sem.at[part, step],
-            recv_sem=recv_sem.at[part, step],
-            device_id=partner(orders[part][step]),
+            dst_ref=table.at[part, pl.ds(start, count)],
+            send_sem=send_sem.at[part, number],
+            recv_sem=recv_sem.at[part, number],
+            device_id=partner(mask),
             device_id_type=MESH,
         )
 
-    def span_of(stage):
-        return (0, 1) if stage == 0 else (1 << (stage - 1), 1 << (stage - 1))
-
-    def hand_over(part, stage):
-        start, count = span_of(stage)
+    def hand_over(part, number):
+        start, count = (0, 1) if number < 0 else pieces[part][number][2:]
         return pltpu.make_async_remote_copy(
             src_ref=table.at[part, pl.ds(start, count)],
             dst_ref=table.at[part, pl.ds(half + start, count)],
-            send_sem=pass_send_sem.at[part, stage],
-            recv_sem=pass_recv_sem.at[part, stage],
-            device_id=partner(orders[part][-1]),
+            send_sem=pass_send_sem.at[part, number + 1],
+            recv_sem=pass_recv_sem.at[part, number + 1],
+            device_id=partner(1 << plan[part][1]),
             device_id_type=MESH,
         )
 
@@ -243,57 +254,71 @@
 
     acc = jnp.zeros((KINDS, batch), f32)
 
-    def arrived(part, step):
-        send(part, step).wait_recv()
-        if step + 1 < steps:
-            send(part, step + 1).start()
-        hand_over(part, step + 1).start()
-
-    events = sorted(
-        ((part * 0.8 + step * 1.8, part, step) for part in range(PARTS) for step in range(steps)),
-    )
-    pending = list(events)
+    def begin(part, stage):
+        for number, piece in enumerate(pieces[part]):
+            if piece[0] == stage:
+                send(part, number).start()
+
+    events = []
+    for part in range(PARTS):
+        for number, (stage, mask, _, _) in enumerate(pieces[part]):
+            when = part * EVERY + stage * STAGE + mask.bit_count() * HOP
+            events.append((when, part, number))
+    events.sort()
+    ready = {}
+
+    def receive(part, number):
+        send(part, number).wait_recv()
+        stage = pieces[part][number][0]
+        ready[part, stage] = ready.get((part, stage), 0) + 1
+        if ready[part, stage] == sum(piece[0] == stage for piece in pieces[part]):
+            begin(part, stage + 1)
+        if plan[part][1] is not None:
+            hand_over(part, number).start()
+
+    taken = []
+    late = []
     for part in range(PARTS):
         load(part).wait()
         evaluate(part)
         if part == 0:
-            pl.semaphore_wait(barrier, len(orders[0]))
-        send(part, 0).start()
-        hand_over(part, 0).start()
-        if part >= 2:
-            _, p, s = pending.pop(0)
-            arrived(p, s)
+            pl.semaphore_wait(barrier, len(partners))
+        begin(part, 0)
+        if plan[part][1] is not None:
+            hand_over(part, -1).start()
+            late.append((part, -1))
+        while events and events[0][0] < (part - 1) * EVERY:
+            _, p, n = events.pop(0)
+            receive(p, n)
+            taken.append((p, n))
     for part in range(PARTS):
         acc = select(acc, part, 0, 1)
-    for part in range(PARTS):
-        hand_over(part, 0).wait_recv()
-        acc = select(acc, part, half, 1)
-    done = [(p, s) for (_, p, s) in events if not any(q[1:] == (p, s) for q in pending)]
-    late = []
-    for p, s in done:
-        start, count = span_of(s + 1)
-        acc = select(acc, p, start, count)
-        late.append((p, s))
-    for _, p, s in pending:
-        arrived(p, s)
-        start, count = span_of(s + 1)
-        acc = select(acc, p, start, count)
-        late.append((p, s))
-        if len(late) > 3:
-            p, s = late.pop(0)
-            hand_over(p, s + 1).wait_recv()
-            start, count = span_of(s + 1)
-            acc = select(acc, p, half + start, count)
-    for p, s in late:
-        hand_over(p, s + 1).wait_recv()
-        start, count = span_of(s + 1)
-        acc = select(acc, p, half + start, count)
+    for p, n in taken:
+        acc = select(acc, p, *pieces[p][n][2:])
+        if plan[p][1] is not None:
+            late.append((p, n))
+
+    def finish(acc, part, number):
+        hand_over(part, number).wait_recv()
+        start, count = (0, 1) if number < 0 else pieces[part][number][2:]
+        return select(acc, part, half + start, count)
+
+    for _, p, n in events:
+        receive(p, n)
+        acc = select(acc, p, *pieces[p][n][2:])
+        if plan[p][1] is not None:
+            late.append((p, n))
+        if len(late) > BEHIND:
+            acc = finish(acc, *late.pop(0))
+    for p, n in late:
+        acc = finish(acc, p, n)
     result_ref[...] = acc
     for part in range(PARTS):
-        for step in range(steps):
-            send(part, step).wait_send()
-        for stage in range(steps + 1):
-            hand_over(part, stage).wait_send()
+        for number in range(len(pieces[part])):
+            send(part, number).wait_send()
+        if plan[part][1] is not None:
+            for number in range(-1, len(pieces[part])):
+                hand_over(part, number).wait_send()
 
 
 def spread(result_ref, q_values_ref, values_ref, targets_ref, q_loss_ref, value_loss_ref):
@@ -312,7 +337,7 @@
     hidden = v_mid.shape[0]
     assert width == LANES and hidden == LANES
     groups = rows_dev // PARTS // LANES
-    steps = log2(owners) - 1
+    sends = max(len(pieces_of(stages)[0]) for stages, _ in plan_of(dp_size, mp_size))
     f32, bf16 = jnp.float32, jnp.bfloat16
     vmem = pl.BlockSpec(memory_space=pltpu.VMEM)
     hbm = pl.BlockSpec(memory_space=pltpu.HBM)
@@ -340,10 +365,10 @@
             pltpu.VMEM((PARTS, KINDS, batch), jnp.int32),
             pltpu.SemaphoreType.DMA((PARTS,)),
             pltpu.SemaphoreType.DMA((8,)),
-            pltpu.SemaphoreType.DMA((PARTS, steps)),
-            pltpu.SemaphoreType.DMA((PARTS, steps)),
-            pltpu.SemaphoreType.DMA((PARTS, steps + 1)),
-            pltpu.SemaphoreType.DMA((PARTS, steps + 1)),
+            pltpu.SemaphoreType.DMA((PARTS, sends)),
+            pltpu.SemaphoreType.DMA((PARTS, sends)),
+            pltpu.SemaphoreType.DMA((PARTS, sends + 1)),
+            pltpu.SemaphoreType.DMA((PARTS, sends + 1)),
         ],
         compiler_params=pltpu.CompilerParams(
             collective_id=0, has_side_effects=True, vmem_limit_bytes=48 << 20

time: 25.9 us -> 22.6 us (0.87)
  Pallas kernels: 25.1 us -> 21.8 us
    pallas_call x1, Pallas kernels: 24.5 us -> 21.2 us  [body(): pl.pallas_call(functools.partial(kernel, dp_size, mp_size), out_shape=plt...]
where the time goes in v3:
time: 22.6 us; the launch traced here: 22.4 us
  Pallas kernels  21.8 us (96%)
  between operations  0.64 us (3%)
    pallas_call x1, Pallas kernels, body(): pl.pallas_call(functools.partial(kernel, dp_size, mp_size), out_shape=plt...  21.2 us
    pallas_call x1, Pallas kernels, body(): pl.pallas_call(spread, out_shape=(two, two, one, one, one), in_specs=[vme...  0.62 us

profile of v3, /device:TPU:0, one launch (start us, length us, event | category | flops | bytes accessed | tf_op | source)
XLA Modules:
  0.0 22.4 jit_solution(6125265382897614039)
XLA Ops:
  0.6 21.2 %critic_exchange.1.result_ref = f32[8,1024]{1,0:T(8,128)S(1)} custom-call(bf16[2048,256]{1,0:T(8,128)(2,1)} %buffer.1, s32[1,1024]{1,0:T(1,128)} %bitcast.7, s32[1,1024]{1,0:T(1,128)} %bitcast.8, bf16[130,2,256]{2,1,0:T(2,128)(2,1)} %bitcast.6, bf16[2,256,256]{2,1,0:T(8,128)(2,1)} %q_mid_hbm.1, bf16[2,256]{1,0:T(2,128)(2,1)} %q_out_hbm.1, ...), custom_call_target="tpu_custom_call" | custom-call | tf_op jit(solution)/shard_map/critic_exchange/pallas_call | solution.py:344
  21.8 0.6 %spread.1 = (f32[2,1024]{1,0:T(2,128)}, f32[2,1024]{1,0:T(2,128)}, f32[1,1024]{1,0:T(1,128)}, f32[1,1024]{1,0:T(1,128)}, f32[1,1024]{1,0:T(1,128)}) custom-call(f32[8,1024]{1,0:T(8,128)S(1)} %critic_exchange.1.result_ref), custom_call_target="tpu_custom_call" | custom-call | tf_op jit(solution)/shard_map/spread/pallas_call | solution.py:395

commit v4 on v3

--- a/solution.py
+++ b/solution.py
@@ -1,4 +1,5 @@
 import functools
+import itertools
 
 import jax
 import jax.numpy as jnp
@@ -11,7 +12,7 @@
 PARTS = 2
 LANES = 256
 KINDS = 8
-EVERY, STAGE, HOP, BEHIND = 0.9, 2.4, 0.8, 6
+EVERY, STAGE, HOP, BEHIND = 0.9, 2.4, 0.8, 2
 
 
 def log2(value):
@@ -25,8 +26,12 @@
     last = mp_bits
     inner = list(range(mp_bits))
     outer = [b for b in range(mp_bits, mp_bits + dp_bits) if b != last]
-    stages = [bits[n : n + 2] for bits in (inner, outer) for n in range(0, len(bits), 2)]
-    return [(stages, last) for _ in range(PARTS)]
+    plan = []
+    for part in range(PARTS):
+        turn = part % max(1, len(outer))
+        pairs = itertools.zip_longest(inner[::-1], outer[turn:] + outer[:turn])
+        plan.append(([[b for b in pair if b is not None] for pair in pairs], last))
+    return plan
 
 
 def pieces_of(stages):
@@ -134,7 +139,7 @@
         wide[0 : value.shape[0], :] = value.astype(f32)
         return wide[...].T
 
-    for fetch in fetches:
+    for fetch in fetches[:6]:
         fetch.wait()
     for head in range(2):
         first_w[head * hidden : (head + 1) * hidden, :] = padded(q_in_ref[:, head, :]).astype(bf16)
@@ -153,23 +158,6 @@
     columns = wide[0:8, :].T
     for head in range(3):
         out_w[head] = jnp.broadcast_to(columns[:, head : head + 1], (hidden, 128))
-
-    wanted = row_ref[...]
-    relative = owner_ref[...] ^ me
-    low = wanted & (LANES - 1)
-    group = wanted // LANES
-    hot[...] = jnp.where(
-        lax.broadcasted_iota(jnp.int32, (LANES, batch), 0) == low, 1.0, 0.0
-    ).astype(bf16)
-    for part in range(PARTS):
-        slot = jnp.zeros_like(relative)
-        stages, last = plan[part]
-        bits = [bit for stage in stages for bit in stage]
-        for position, bit in enumerate(bits + ([] if last is None else [last])):
-            slot = slot + (((relative >> bit) & 1) << position)
-        here = (group // groups) == part
-        index = jnp.where(here, slot * groups + (group - part * groups), -1)
-        place[part] = jnp.broadcast_to(index, (KINDS, batch))
 
     def send(part, number):
         _, mask, start, count = pieces[part][number]
@@ -291,6 +279,25 @@
             _, p, n = events.pop(0)
             receive(p, n)
             taken.append((p, n))
+    for fetch in fetches[6:]:
+        fetch.wait()
+    wanted = row_ref[...]
+    relative = owner_ref[...] ^ me
+    low = wanted & (LANES - 1)
+    group = wanted // LANES
+    hot[...] = jnp.where(
+        lax.broadcasted_iota(jnp.int32, (LANES, batch), 0) == low, 1.0, 0.0
+    ).astype(bf16)
+    for part in range(PARTS):
+        slot = jnp.zeros_like(relative)
+        stages, last = plan[part]
+        bits = [bit for stage in stages for bit in stage]
+        for position, bit in enumerate(bits + ([] if last is None else [last])):
+            slot = slot + (((relative >> bit) & 1) << position)
+        here = (group // groups) == part
+        index = jnp.where(here, slot * groups + (group - part * groups), -1)
+        place[part] = jnp.broadcast_to(index, (KINDS, batch))
+
     for part in range(PARTS):
         acc = select(acc, part, 0, 1)
     for p, n in taken:

time: 22.6 us -> 21.2 us (0.938)
  Pallas kernels: 21.8 us -> 20.4 us
    pallas_call x1, Pallas kernels: 21.2 us -> 19.8 us  [body(): pl.pallas_call(functools.partial(kernel, dp_size, mp_size), out_shape=plt...]
where the time goes in v4:
time: 21.2 us; the launch traced here: 21 us
  Pallas kernels  20.4 us (96%)
  between operations  0.64 us (3%)
    pallas_call x1, Pallas kernels, body(): pl.pallas_call(functools.partial(kernel, dp_size, mp_size), out_shape=plt...  19.8 us
    pallas_call x1, Pallas kernels, body(): pl.pallas_call(spread, out_shape=(two, two, one, one, one), in_specs=[vme...  0.62 us

profile of v4, /device:TPU:0, one launch (start us, length us, event | category | flops | bytes accessed | tf_op | source)
XLA Modules:
  0.0 21.0 jit_solution(3984994085752785589)
XLA Ops:
  0.6 19.8 %critic_exchange.1.result_ref = f32[8,1024]{1,0:T(8,128)S(1)} custom-call(bf16[2048,256]{1,0:T(8,128)(2,1)} %buffer.1, s32[1,1024]{1,0:T(1,128)} %bitcast.7, s32[1,1024]{1,0:T(1,128)} %bitcast.8, bf16[130,2,256]{2,1,0:T(2,128)(2,1)} %bitcast.6, bf16[2,256,256]{2,1,0:T(8,128)(2,1)} %q_mid_hbm.1, bf16[2,256]{1,0:T(2,128)(2,1)} %q_out_hbm.1, ...), custom_call_target="tpu_custom_call" | custom-call | tf_op jit(solution)/shard_map/critic_exchange/pallas_call | solution.py:351
  20.4 0.6 %spread.1 = (f32[2,1024]{1,0:T(2,128)}, f32[2,1024]{1,0:T(2,128)}, f32[1,1024]{1,0:T(1,128)}, f32[1,1024]{1,0:T(1,128)}, f32[1,1024]{1,0:T(1,128)}) custom-call(f32[8,1024]{1,0:T(8,128)S(1)} %critic_exchange.1.result_ref), custom_call_target="tpu_custom_call" | custom-call | tf_op jit(solution)/shard_map/spread/pallas_call | solution.py:402
